TPU v7x, 32 devices: a whole 2x2x4 slice. The times are simulated.
32 devices in a mesh: ctx: 16 (over z, y, core), head: 2 (over x).
Axes of the slice: x: 2, y: 2, z: 4, core: 2. Of those that a mesh axis runs over, the one named last changes fastest.
Arguments:
- fine_query: bfloat16 [4096, 4096], P('ctx', 'head'), may hold values from -181 to 181
- fine_memory: bfloat16 [2, 4096, 1024], P(None, 'ctx', 'head'), may hold values from -6.5 to 6.5
- coarse_query: bfloat16 [2048, 4096], P('ctx', 'head'), may hold values from -181 to 181
- coarse_memory: bfloat16 [2, 2048, 1024], P(None, 'ctx', 'head'), may hold values from -6.5 to 6.5
- coarse_scale: int32 [2048], P('ctx'), may hold values from 0 to 7, never falling along the last dimension, each value on 1 to 512 neighbouring positions
- out_weight: bfloat16 [4096, 4096], P('head'), may hold values from -0.09375 to 0.09375
Outputs:
- fine_mixed: bfloat16 [4096, 4096], P(('ctx', 'head'))
- coarse_mixed: bfloat16 [2048, 4096], P(('ctx', 'head'))
Inputs may be any that keep to these rules, and one draw needn't show every extreme that they name: `coarse_scale`: never falls along the coarse tokens.
All inputs are finite; a program needn't handle non-finite values.
Results may differ from a plain program's by a relative error of at most 0.014.
Values may be sent and summed in bfloat16 or wider, within the bound.
A program may use at most 128 MiB of HBM per device.

v0:
```python
import functools
import math

import jax
import jax.numpy as jnp
from jax import lax
from jax.experimental import pallas as pl
from jax.experimental.pallas import tpu as pltpu
from jax.sharding import PartitionSpec as P

HD = 128
MASKED = -1e30
LOG2E = math.log2(math.e)


def split_queries(rows):
    scaled = rows.astype(jnp.float32) * (HD ** (-0.5) * LOG2E)
    high = scaled.astype(jnp.bfloat16)
    low = (scaled - high.astype(jnp.float32)).astype(jnp.bfloat16)
    return jnp.concatenate([high, low], axis=1)


def scores_of(keys, pair):
    doubled = jnp.concatenate([keys, keys], axis=1)
    return lax.dot_general(
        doubled, pair, (((1,), (1,)), ((), ())), preferred_element_type=jnp.float32
    )


def fold(state, scores, values_t):
    highest, total, weighted = state
    new = jnp.maximum(highest, jnp.max(scores, axis=0, keepdims=True))
    rescale = jnp.exp2(highest - new)
    shifted = jnp.exp2(scores - new)
    total = total * rescale + jnp.sum(shifted, axis=0, keepdims=True)
    weighted = weighted * rescale + jnp.dot(
        values_t, shifted.astype(jnp.bfloat16), preferred_element_type=jnp.float32
    )
    return (new, total, weighted)


def start(columns):
    return (
        jnp.full((1, columns), MASKED, jnp.float32),
        jnp.zeros((1, columns), jnp.float32),
        jnp.zeros((HD, columns), jnp.float32),
    )


def fill_values(kv_ref, vt_ref, span):
    for at in range(0, kv_ref.shape[1], span):
        vt_ref[:, at : at + span] = kv_ref[1, at : at + span, :].T


def run(kv_ref, vt_ref, span, pair, state, allowed):
    def scored(at):
        return allowed(scores_of(kv_ref[0, at : at + span, :], pair), at)

    places = list(range(0, kv_ref.shape[1], span))
    ahead = scored(places[0])
    for which, at in enumerate(places):
        scores = ahead
        if which + 1 < len(places):
            ahead = scored(places[which + 1])
        state = fold(state, scores, vt_ref[:, at : at + span])
    return state


def finish(state):
    return (state[2] / state[1]).T.astype(jnp.bfloat16)


def head_columns(head):
    return pl.ds(pl.multiple_of(head * HD, HD), HD)


def unmasked(scores, at):
    return scores


def coarse_kernel(
    ratio, span, fq_ref, cq_ref, kv_ref, qlev_ref, klev_ref, co_ref, stat_ref, sum_ref, vt_ref
):
    coarse_rows = cq_ref.shape[0]
    fill_values(kv_ref, vt_ref, span)
    stack = 2 if ratio % 2 == 0 else 1
    levels = jnp.concatenate([qlev_ref[...]] * stack, axis=1)

    def masked(scores, at):
        return jnp.where(klev_ref[at : at + span, :] <= levels, scores, MASKED)

    @pl.loop(0, ratio // stack)
    def _(part):
        heads = [head_columns(part * stack + i) for i in range(stack)]
        pair = jnp.concatenate([split_queries(cq_ref[:, columns]) for columns in heads], axis=0)
        result = finish(run(kv_ref, vt_ref, span, pair, start(pair.shape[0]), masked))
        for i, columns in enumerate(heads):
            co_ref[:, columns] = result[i * coarse_rows : (i + 1) * coarse_rows]

    @pl.loop(0, ratio)
    def _(head):
        pair = split_queries(fq_ref[:, head_columns(head)])
        state = run(kv_ref, vt_ref, span, pair, start(pair.shape[0]), unmasked)
        stat_ref[head] = jnp.concatenate([state[0], state[1]], axis=0)
        sum_ref[head] = state[2]


def fine_kernel(ratio, span, last, fq_ref, kv_ref, stat_in, sum_in, *rest):
    vt_ref = rest[-1]
    fill_values(kv_ref, vt_ref, span)

    @pl.loop(0, ratio)
    def _(head):
        pair = split_queries(fq_ref[:, head_columns(head)])
        stat = stat_in[head]
        state = run(kv_ref, vt_ref, span, pair, (stat[0:1], stat[1:2], sum_in[head]), unmasked)
        if last:
            rest[0][:, head_columns(head)] = finish(state)
        else:
            rest[0][head] = jnp.concatenate([state[0], state[1]], axis=0)
            rest[1][head] = state[2]


def cost_of(rows, keys, width):
    pairs = rows * keys * (width // HD)
    return pl.CostEstimate(
        flops=8 * pairs * HD, transcendentals=pairs, bytes_accessed=4 * (rows + keys) * width
    )


def specs_of(rows, ratio):
    width = ratio * HD
    query = pl.BlockSpec((rows, width), lambda g: (0, g))
    stat = pl.BlockSpec((ratio, 2, rows), lambda g: (g, 0, 0))
    sums = pl.BlockSpec((ratio, HD, rows), lambda g: (g, 0, 0))
    return query, stat, sums


def state_shapes(heads, rows):
    return (
        jax.ShapeDtypeStruct((heads, 2, rows), jnp.float32),
        jax.ShapeDtypeStruct((heads, HD, rows), jnp.float32),
    )


def memory_spec(keys):
    return pl.BlockSpec((2, keys, HD), lambda g: (0, 0, g))


def coarse_part(fine_query, coarse_query, kv, query_levels, key_levels):
    keys, groups = kv.shape[1], kv.shape[2] // HD
    heads = fine_query.shape[1] // HD
    ratio = heads // groups
    rows, coarse_rows = fine_query.shape[0], coarse_query.shape[0]
    query, stat, sums = specs_of(rows, ratio)
    coarse = pl.BlockSpec((coarse_rows, ratio * HD), lambda g: (0, g))
    return pl.pallas_call(
        functools.partial(coarse_kernel, ratio, math.gcd(keys, 512)),
        grid=(groups,),
        out_shape=(
            jax.ShapeDtypeStruct(coarse_query.shape, jnp.bfloat16),
            *state_shapes(heads, rows),
        ),
        in_specs=[
            query,
            coarse,
            memory_spec(keys),
            pl.BlockSpec((1, coarse_rows), lambda g: (0, 0)),
            pl.BlockSpec((keys, 1), lambda g: (0, 0)),
        ],
        out_specs=(coarse, stat, sums),
        scratch_shapes=[pltpu.VMEM((HD, keys), jnp.bfloat16)],
        compiler_params=pltpu.CompilerParams(vmem_limit_bytes=48 << 20),
        cost_estimate=cost_of(rows + coarse_rows, keys, heads * HD),
    )(fine_query, coarse_query, kv, query_levels, key_levels)


def fine_part(fine_query, kv, state, last):
    keys, groups = kv.shape[1], kv.shape[2] // HD
    heads = fine_query.shape[1] // HD
    ratio = heads // groups
    rows = fine_query.shape[0]
    query, stat, sums = specs_of(rows, ratio)
    if last:
        shapes = jax.ShapeDtypeStruct(fine_query.shape, jnp.bfloat16)
    else:
        shapes = state_shapes(heads, rows)
    return pl.pallas_call(
        functools.partial(fine_kernel, ratio, math.gcd(keys, 512), last),
        grid=(groups,),
        out_shape=shapes,
        in_specs=[query, memory_spec(keys), stat, sums],
        out_specs=query if last else (stat, sums),
        scratch_shapes=[pltpu.VMEM((HD, keys), jnp.bfloat16)],
        compiler_params=pltpu.CompilerParams(vmem_limit_bytes=48 << 20),
        cost_estimate=cost_of(rows, keys, heads * HD),
    )(fine_query, kv, *state)


def gathered(memory):
    return lax.all_gather(memory, "ctx", axis=1, tiled=True)


def per_device(fine_query, fine_memory, coarse_query, coarse_memory, coarse_scale, out_weight):
    levels = coarse_scale.astype(jnp.float32)
    key_levels = lax.all_gather(
        levels.astype(jnp.bfloat16).reshape(1, -1), "ctx", axis=1, tiled=True
    )
    pieces = 2 if fine_memory.shape[1] % 256 == 0 else 1
    coarse_kv = gathered(coarse_memory)
    fine_kvs = [gathered(piece) for piece in jnp.split(fine_memory, pieces, axis=1)]
    coarse_attention, *state = coarse_part(
        fine_query,
        coarse_query,
        coarse_kv,
        levels.reshape(1, -1),
        key_levels.astype(jnp.float32).reshape(-1, 1),
    )

    def mix(rows):
        partial = jnp.dot(rows, out_weight, preferred_element_type=jnp.float32)
        return lax.psum_scatter(
            partial.astype(jnp.bfloat16), "head", scatter_dimension=0, tiled=True
        )

    coarse_mixed = mix(coarse_attention)
    for kv in fine_kvs[:-1]:
        state = fine_part(fine_query, kv, state, False)
    return (mix(fine_part(fine_query, fine_kvs[-1], state, True)), coarse_mixed)


def solution(mesh):
    placed = (
        P("ctx", "head"),
        P(None, "ctx", "head"),
        P("ctx", "head"),
        P(None, "ctx", "head"),
        P("ctx"),
        P("head", None),
    )
    return jax.shard_map(
        per_device,
        mesh=mesh,
        in_specs=placed,
        out_specs=(P(("ctx", "head"), None), P(("ctx", "head"), None)),
        check_vma=False,
    )
```

profile of v0, /device:TPU:0, one launch (start us, length us, event | category | flops | bytes accessed | tf_op | source)
XLA Modules:
  0.0 234.4 jit_solution(8382480680707840682)
XLA Ops:
  7.2 0.0 all-gather.10.cloned.1.call-start
  7.2 0.7 all-gather.10.cloned.1.call-update
  7.9 0.0 all-gather.8.cloned.1.call-start
  7.9 1.9 fusion
  9.8 0.0 all-gather.8.cloned.1.call-update
  9.8 0.0 all-gather.6.cloned.1.call-start
  9.9 0.7 all-gather.6.cloned.1.call-update
  10.6 0.0 reduce-scatter.5.cloned.1.call-start
  10.6 0.7 convert_bitcast_fusion
  11.3 23.2 %all-gather.1 = bf16[16,1,128]{2,1,0:T(2,128)(2,1)S(1)} all-gather(bf16[1,1,128]{2,1,0:T(2,128)(2,1)S(1)} %get-tuple-element.14), channel_id=2, replica_groups=mesh['ctx'=16,'head'=2] {'ctx'}, dimensions={0}, use_global_device_ids=true | all-gather | bytes 4352 | tf_op jit(solution)/shard_map/all_gather | solution.py:206
  34.5 0.4 copy.10.klev_ref
  34.9 28.5 %all-gather.10.cloned.1.call-done.kv_ref = bf16[2,2048,512]{2,1,0:T(8,128)(2,1)} async-done(((bf16[2,128,512]{2,1,0:T(8,128)(2,1)}), bf16[2,2048,512]{2,1,0:T(8,128)(2,1)}) %all-gather.10.cloned.1.call-update) | async-done | bytes 4194320 | tf_op jit(solution)/shard_map/all_gather | solution.py:201
  63.4 0.0 copy-start
  63.4 1.2 copy-done
  64.6 0.0 copy-start.2
  64.6 1.0 copy-done.2
  65.7 27.3 %shard_map.77 = (bf16[128,2048]{1,0:T(8,128)(2,1)S(1)}, f32[16,2,256]{2,1,0:T(2,128)S(1)}, f32[16,128,256]{2,1,0:T(8,128)S(1)}) custom-call(bf16[256,2048]{1,0:T(8,128)(2,1)S(1)} %copy-done, bf16[128,2048]{1,0:T(8,128)(2,1)S(1)} %copy-done.2, bf16[2,2048,512]{2,1,0:T(8,128)(2,1)} %all-gather.10.cloned.1.call-done.kv_ref, ...), custom_call_target="tpu_custom_call" | custom-call | flops 12884901888 | bytes 19922944 | tf_op jit(solution)/shard_map/pallas_call | solution.py:157
  93.0 0.0 copy-start.3
  93.0 1.4 copy-done.3
  94.4 9.3 %convolution_convert_fusion.1 = bf16[128,4096]{1,0:T(8,128)(2,1)} fusion(bf16[128,2048]{1,0:T(8,128)(2,1)S(1)} %get-tuple-element.11, bf16[2048,4096]{1,0:T(8,128)(2,1)} %param.11), kind=kOutput, calls=%fused_computation.1 | convolution fusion | flops 2148007936 | bytes 18350080 | tf_op jit(solution)/shard_map/dot_general | solution.py:221
  103.6 0.0 reduce-scatter.5.cloned.1.call-update
  103.6 0.0 reduce-scatter.3.cloned.1.call-start
  103.7 11.5 %all-gather.8.cloned.1.call-done.kv_ref = bf16[2,2048,512]{2,1,0:T(8,128)(2,1)} async-done(((bf16[2,128,512]{2,1,0:T(8,128)(2,1)}), bf16[2,2048,512]{2,1,0:T(8,128)(2,1)}) %all-gather.8.cloned.1.call-update) | async-done | bytes 4194320 | tf_op jit(solution)/shard_map/all_gather | solution.py:201
  115.2 0.0 copy-done.1
  115.2 1.6 copy-done.4
  116.8 18.1 %shard_map.78 = (f32[16,2,256]{2,1,0:T(2,128)S(1)}, f32[16,128,256]{2,1,0:T(8,128)S(1)}) custom-call(bf16[256,2048]{1,0:T(8,128)(2,1)S(1)} %copy-done.1, bf16[2,2048,512]{2,1,0:T(8,128)(2,1)} %all-gather.8.cloned.1.call-done.kv_ref, f32[16,2,256]{2,1,0:T(2,128)S(1)} %get-tuple-element.7.stat_in, f32[16,128,256]{2,1,0:T(8,128)S(1)} %copy-done.4), custom_call_target="tpu_custom_call" | custom-call | flops 8589934592 | bytes 18874368 | tf_op jit(solution)/shard_map/pallas_call | solution.py:188
  134.9 31.5 %all-gather.6.cloned.1.call-done.kv_ref = bf16[2,2048,512]{2,1,0:T(8,128)(2,1)} async-done(((bf16[2,128,512]{2,1,0:T(8,128)(2,1)}), bf16[2,2048,512]{2,1,0:T(8,128)(2,1)}) %all-gather.6.cloned.1.call-update) | async-done | bytes 4194320 | tf_op jit(solution)/shard_map/all_gather | solution.py:201
  166.4 19.3 %shard_map.79 = bf16[256,2048]{1,0:T(8,128)(2,1)S(1)} custom-call(bf16[256,2048]{1,0:T(8,128)(2,1)S(1)} %copy-done.1, bf16[2,2048,512]{2,1,0:T(8,128)(2,1)} %all-gather.6.cloned.1.call-done.kv_ref, f32[16,2,256]{2,1,0:T(2,128)S(1)} %get-tuple-element.9.stat_in, f32[16,128,256]{2,1,0:T(8,128)S(1)} %get-tuple-element.10.sum_in), custom_call_target="tpu_custom_call" | custom-call | flops 8589934592 | bytes 18874368 | tf_op jit(solution)/shard_map/pallas_call | solution.py:188
  185.7 11.5 %convolution_convert_fusion = bf16[256,4096]{1,0:T(8,128)(2,1)} fusion(bf16[256,2048]{1,0:T(8,128)(2,1)S(1)} %shard_map.79, bf16[2048,4096]{1,0:T(8,128)(2,1)} %param.11), kind=kOutput, calls=%fused_computation | convolution fusion | flops 4296015872 | bytes 19922944 | tf_op jit(solution)/shard_map/dot_general | solution.py:221
  197.2 0.0 reduce-scatter.3.cloned.1.call-update
  197.3 0.0 reduce-scatter.5.cloned.1.call-done
  197.3 30.6 %reduce-scatter.3.cloned.1.call-done = bf16[128,4096]{1,0:T(8,128)(2,1)} async-done(((bf16[256,4096]{1,0:T(8,128)(2,1)}), bf16[128,4096]{1,0:T(8,128)(2,1)}) %reduce-scatter.3.cloned.1.call-update) | async-done | bytes 1048592 | tf_op jit(solution)/shard_map/reduce_scatter | solution.py:222
  (3 shorter events, 0.0 us)
Async XLA Ops:
  7.2 56.2 %all-gather.10.cloned.1.call-start = ((), (), s32[]{:S(2)}) async-start(), calls=%async_computation.4 | async-start | bytes 4456448 | tf_op jit(solution)/shard_map/all_gather | solution.py:201
  7.9 107.3 %all-gather.8.cloned.1.call-start = ((), (), s32[]{:S(2)}) async-start(), calls=%async_computation.3 | async-start | bytes 4456448 | tf_op jit(solution)/shard_map/all_gather | solution.py:201
  9.8 156.6 %all-gather.6.cloned.1.call-start = ((), (), s32[]{:S(2)}) async-start(), calls=%async_computation.2 | async-start | bytes 4456448 | tf_op jit(solution)/shard_map/all_gather | solution.py:201
  10.6 186.7 %reduce-scatter.5.cloned.1.call-start = ((), (), s32[]{:S(2)}) async-start(), calls=%async_computation.6 | async-start | bytes 1572864 | tf_op jit(solution)/shard_map/reduce_scatter | solution.py:222
  63.4 1.2 copy-start
  64.6 1.0 copy-start.2
  93.0 1.4 copy-start.3
  94.4 20.9 %copy-start.1 = (bf16[256,2048]{1,0:T(8,128)(2,1)S(1)}, bf16[256,2048]{1,0:T(8,128)(2,1)}, u32[]{:S(2)}) copy-start(bf16[256,2048]{1,0:T(8,128)(2,1)} %fq_ref.5) | copy-start | bytes 3145732
  103.6 124.2 %reduce-scatter.3.cloned.1.call-start = ((), (), s32[]{:S(2)}) async-start(), calls=%async_computation.5 | async-start | bytes 3145728 | tf_op jit(solution)/shard_map/reduce_scatter | solution.py:222
  115.2 1.6 copy-start.4
Sparse Core Ops, SparseCore 0:
  10.2 53.1 all-gather.9
  66.1 49.0 all-gather.7
  117.4 48.9 all-gather.5
  169.1 18.9 reduce-scatter.4
  197.4 30.4 reduce-scatter.2
where the time goes:
time: 235 us; the launch traced here: 234 us
  waiting for transfers between devices  103 us (44%)
  Pallas kernels  64.7 us (28%)
  blocking collectives  23.2 us (10%)
  matrix products  20.8 us (9%)
  between operations  13.8 us (6%)
  local copies, waits for them, and re-layouts  7.49 us (3%)
    all_gather x3, waiting for transfers between devices, gathered(): return lax.all_gather(memory, 'ctx', axis=1, tiled=True)  71.5 us
    pallas_call x2, Pallas kernels, fine_part(): pl.pallas_call(functools.partial(fine_kernel, ratio, math.gcd(keys, 512),...  37.4 us
    reduce_scatter x2, waiting for transfers between devices, mix(): lax.psum_scatter(partial.astype(jnp.bfloat16), 'head', scatter_dimension=...  30.6 us
    pallas_call x1, Pallas kernels, coarse_part(): pl.pallas_call(functools.partial(coarse_kernel, ratio, math.gcd(keys, 512...  27.3 us
    all_gather x1, blocking collectives, per_device(): lax.all_gather(levels.astype(jnp.bfloat16).reshape(1, -1), 'ctx', axis=1,...  23.2 us
    dot_general x2, matrix products, mix(): partial = jnp.dot(rows, out_weight, preferred_element_type=jnp.float32)  20.8 us
    unnamed x10, local copies, waits for them, and re-layouts  5.24 us
  transfers between devices with their start and end apart: 5, of which 4 were waited for; matrix products, arithmetic and copies ran while one was open for 10% of the time, Pallas kernels for 28%

commit v1 on v0

v1 whole, which is shorter than its diff:
```python
import functools
import math

import jax
import jax.numpy as jnp
from jax import lax
from jax.experimental import pallas as pl
from jax.experimental.pallas import tpu as pltpu
from jax.sharding import PartitionSpec as P

HD = 128
MASKED = -1e30
LOG2E = math.log2(math.e)
MESH = pl.DeviceIdType.MESH
PAIR, CORES = 2, 2
TILE = 512


def line_is_outer(mesh):
    chips = mesh.devices.reshape(mesh.devices.shape[0], -1)[::CORES, 0]
    try:
        places = [tuple(chip.coords) for chip in chips]
    except (AttributeError, TypeError):
        return True
    fast = [i for i in range(3) if places[0][i] != places[1][i]]
    run = 1
    while run < len(places) and all(
        places[run][i] == places[0][i] for i in range(3) if i not in fast
    ):
        run += 1
    return run == PAIR or len(places) != PAIR * run


def split_queries(rows):
    scaled = rows.astype(jnp.float32) * (HD ** (-0.5) * LOG2E)
    high = scaled.astype(jnp.bfloat16)
    low = (scaled - high.astype(jnp.float32)).astype(jnp.bfloat16)
    return jnp.concatenate([high, low], axis=1)


def scores_of(keys, pair):
    doubled = jnp.concatenate([keys, keys], axis=1)
    return lax.dot_general(
        doubled, pair, (((1,), (1,)), ((), ())), preferred_element_type=jnp.float32
    )


def fold(state, scores, values_t):
    highest, total, weighted = state
    new = jnp.maximum(highest, jnp.max(scores, axis=0, keepdims=True))
    rescale = jnp.exp2(highest - new)
    shifted = jnp.exp2(scores - new)
    total = total * rescale + jnp.sum(shifted, axis=0, keepdims=True)
    weighted = weighted * rescale + jnp.dot(
        values_t, shifted.astype(jnp.bfloat16), preferred_element_type=jnp.float32
    )
    return (new, total, weighted)


def columns_of(head):
    return pl.ds(pl.multiple_of(head * HD, HD), HD)


def schedule_of(line, pieces):
    coarse = [(d, 0) for d in range(1, line)]
    fine = [(d, p) for d in range(1, line) for p in range(1, pieces)]
    takes, rest = [coarse[0]], coarse[1:]
    while rest or fine:
        if rest:
            takes.append(rest.pop(0))
        if fine:
            takes.append(fine.pop(0))
    own = [(0, p) for p in range(pieces)]
    uses = own[:2] + takes[:1] + own[2:] + takes[1:]
    steps = [("O", u) for u in own[:2]] + [("T", takes[0])] + [("O", u) for u in own[2:]]
    steps += [("U", u) for u in uses[:2]]
    takes, uses = takes[1:], uses[2:]
    for count in [2, 2] + [1] * len(takes):
        steps += [("T", u) for u in takes[:count]]
        takes = takes[count:]
        for u in uses[: count if len(steps) < 12 else 1]:
            steps.append(("U", u))
        uses = uses[count if len(steps) < 12 else 1 :]
    steps += [("T", u) for u in takes] + [("U", u) for u in uses]
    order, done = [], False
    for at, step in enumerate(steps):
        order.append(step)
        if step == ("U", (line - 1, 0)):
            order.append(("C", None))
    return order


def kernel(
    line, outer, heads_axis, ratio,
    fq_hbm, cq_hbm, fm_hbm, cm_hbm, lev_hbm, w_hbm,
    fo_hbm, co_hbm,
    kv, lev, klev, fq, cq, fpair, cpair, vt, facc, fstat, cacc, cstat,
    fatt, catt, w, fmine, cmine, fsend, csend, frecv, crecv, fout, cout,
    zr, zs, yr, ys, cr, cs, hs, hr, loc, outs,
):
    keys = cm_hbm.shape[1]
    pieces = 1 + fm_hbm.shape[1] // keys
    groups = kv.shape[3] // HD
    rows, crows = fq.shape[0], cq.shape[0]
    unit = PAIR * CORES * keys
    part, cpart = rows // heads_axis, crows // heads_axis
    width = w.shape[1]
    tiles = width // TILE

    me, head = lax.axis_index("ctx"), lax.axis_index("head")
    core = lax.rem(me, CORES)
    if outer:
        pair, place = lax.rem(me // CORES, PAIR), me // (CORES * PAIR)
    else:
        pair, place = me // (CORES * line), lax.rem(me // CORES, line)

    def device(l, q, c):
        index = (l * PAIR + q) * CORES + c if outer else (q * line + l) * CORES + c
        return (index, head)

    def slot(l, q, c):
        return (l * PAIR + q) * CORES + c

    def span(l, q, c):
        return pl.ds(pl.multiple_of(slot(l, q, c) * keys, keys), keys)

    right, left = device(place + 1, pair, core), device(place - 1, pair, core)
    across, beside = device(place, 1 - pair, core), device(place, pair, 1 - core)
    has_right, has_left = place + 1 < line, place > 0
    others = [lax.rem(head + k, heads_axis) for k in range(1, heads_axis)]

    def greet(target):
        pl.semaphore_signal(barrier, inc=1, device_id=target, device_id_type=MESH)

    barrier = pltpu.get_barrier_semaphore()
    pl.when(has_right)(lambda: greet(right))
    pl.when(has_left)(lambda: greet(left))
    greet(across)
    greet(beside)
    for other in others:
        greet((me, other))

    def held(l, q, c, p):
        if p == pieces:
            return lev.at[slot(l, q, c)]
        return kv.at[p, :, span(l, q, c), :]

    def own_source(p):
        if p == pieces:
            return lev_hbm
        if p == 0:
            return cm_hbm
        return fm_hbm.at[:, (p - 1) * keys : p * keys, :]

    def along(p):
        return [p, pieces] if p == 0 else [p]

    own_copies = [
        pltpu.make_async_copy(own_source(p), held(place, pair, core, p), loc.at[p])
        for p in range(pieces + 1)
    ]
    q_copies = [
        pltpu.make_async_copy(fq_hbm, fq, loc.at[pieces + 1]),
        pltpu.make_async_copy(cq_hbm, cq, loc.at[pieces + 2]),
    ]
    w_copy = pltpu.make_async_copy(w_hbm, w, loc.at[pieces + 3])
    for copy in q_copies + own_copies:
        copy.start()

    def remote(source, l, q, c, p, send, recv, target):
        return pltpu.make_async_remote_copy(
            src_ref=source,
            dst_ref=held(l, q, c, p),
            send_sem=send,
            recv_sem=recv,
            device_id=target,
            device_id_type=MESH,
        )

    def to_line(l, p, way, target, source=None):
        source = held(l, pair, core, p) if source is None else source
        return remote(source, l, pair, core, p, zs.at[way, l, p], zr.at[l, p], target)

    def to_pair(l, p, source=None):
        source = held(l, pair, core, p) if source is None else source
        return remote(source, l, pair, core, p, ys.at[l, p], yr.at[l, p], across)

    def to_core(l, q, p, source=None):
        source = held(l, q, core, p) if source is None else source
        return remote(source, l, q, core, p, cs.at[l, q, p], cr.at[l, q, p], beside)

    def from_line(l, p):
        return remote(
            held(l, pair, core, p), l, pair, core, p, zs.at[0, l, p], zr.at[l, p], across
        )

    def from_pair(l, p):
        at = held(l, 1 - pair, core, p)
        return remote(at, l, 1 - pair, core, p, ys.at[l, p], yr.at[l, p], across)

    def from_core(l, q, p):
        at = held(l, q, 1 - core, p)
        return remote(at, l, q, 1 - core, p, cs.at[l, q, p], cr.at[l, q, p], beside)

    def send_own(p):
        for a in along(p):
            source = own_source(a)
            pl.when(has_right)(lambda: to_line(place, a, 0, right, source).start())
            pl.when(has_left)(lambda: to_line(place, a, 1, left, source).start())
            to_pair(place, a, source).start()
            to_core(place, pair, a, source).start()

    def sides(d):
        if d == 0:
            return [(place, None, None)]
        return [(place - d, place >= d, 0), (place + d, place + d < line, 1)]

    def take_line(d, p):
        for l, valid, way in sides(d):
            onward = has_right if way == 0 else has_left

            @pl.when(valid)
            def _():
                for a in along(p):
                    from_line(l, a).wait_recv()
                    target = right if way == 0 else left
                    pl.when(onward)(lambda: to_line(l, a, way, target).start())
                    to_pair(l, a).start()
                    to_core(l, pair, a).start()

    def take_pair(l, p):
        for a in along(p):
            from_pair(l, a).wait_recv()
            to_core(l, 1 - pair, a).start()

    def step(pair_ref, acc_ref, stat_ref, at, scores, values_t):
        stat = stat_ref[at]
        new, total, weighted = fold((stat[0:1], stat[1:2], acc_ref[at]), scores, values_t)
        stat_ref[at, 0:1] = new
        stat_ref[at, 1:2] = total
        acc_ref[at] = weighted

    cstack = cpair.shape[1] // crows

    def use(l, p):
        base = pl.multiple_of(l * unit, unit)

        @pl.loop(0, groups)
        def _(g):
            vt[...] = kv[p, 1, pl.ds(base, unit), columns_of(g)].T

            @pl.loop(0, ratio // 2)
            def _(h):
                block = kv[p, 0, pl.ds(base, unit), columns_of(g)]
                ats = [g * ratio + h * 2 + k for k in range(2)]
                scores = [scores_of(block, fpair[at]) for at in ats]
                for at, score in zip(ats, scores):
                    step(fpair, facc, fstat, at, score, vt[...])

            if p == 0:
                @pl.loop(0, ratio // cstack)
                def _(h):
                    block = kv[p, 0, pl.ds(base, unit), columns_of(g)]
                    at = g * (ratio // cstack) + h
                    level = klev[pl.ds(base, unit), :]
                    mine = jnp.max(lev[slot(place, pair, core)], axis=0, keepdims=True)
                    allowed = jnp.concatenate([level <= mine] * cstack, axis=1)
                    scores = jnp.where(allowed, scores_of(block, cpair[at]), MASKED)
                    step(cpair, cacc, cstat, at, scores, vt[...])

    def take(d, p):
        if d == 0:
            own_copies[p].wait()
            if p == 0:
                own_copies[pieces].wait()
        for l, valid, way in sides(d):

            def body():
                take_pair(l, p)
                for a in along(p):
                    for q in range(PAIR):
                        from_core(l, q, a).wait_recv()
                if p == 0:
                    for q in range(PAIR):
                        for c in range(CORES):
                            column = lev[slot(l, q, c)].T[:, 0:1]
                            klev[span(l, q, c), :] = jnp.broadcast_to(column, (keys, crows))

            if valid is None:
                body()
            else:
                pl.when(valid)(body)

        if d == 0:
            use(place, p)
        else:

            @pl.loop(0, 2)
            def _(way):
                l = place + (2 * way - 1) * d

                @pl.when(jnp.logical_and(l >= 0, l < line))
                def _():
                    use(l, p)

    def finish(acc, stat):
        return (acc / stat[1:2]).T.astype(jnp.bfloat16)

    def rotated(block):
        return lax.rem(block + heads_axis - head, heads_axis)

    def finish_coarse():
        @pl.loop(0, groups * ratio // cstack)
        def _(at):
            result = finish(cacc[at], cstat[at])
            for k in range(cstack):
                for b in range(heads_axis):
                    to = pl.multiple_of(rotated(b) * cpart, cpart)
                    lo = k * crows + b * cpart
                    catt[pl.ds(to, cpart), columns_of(at * cstack + k)] = result[lo : lo + cpart]

    def finish_fine():
        @pl.loop(0, groups * ratio)
        def _(at):
            result = finish(facc[at], fstat[at])
            for b in range(heads_axis):
                to = pl.multiple_of(rotated(b) * part, part)
                fatt[pl.ds(to, part), columns_of(at)] = result[b * part : (b + 1) * part]

    def share(which, k, t):
        size, send, recv = ((part, fsend, frecv), (cpart, csend, crecv))[which]
        return pltpu.make_async_remote_copy(
            src_ref=send.at[k, t],
            dst_ref=recv.at[k, t],
            send_sem=hs.at[which, k, t],
            recv_sem=hr.at[which, k, t],
            device_id=(me, others[k]),
            device_id_type=MESH,
        )

    def project(which):
        att, mine, send, size = ((fatt, fmine, fsend, part), (catt, cmine, csend, cpart))[which]

        @pl.loop(0, tiles)
        def _(t):
            piece = w[:, pl.ds(pl.multiple_of(t * TILE, TILE), TILE)]
            result = jnp.dot(att[...], piece, preferred_element_type=jnp.float32)
            mine[t] = result[:size]
            for k in range(heads_axis - 1):
                send[k, t] = result[(k + 1) * size : (k + 2) * size].astype(jnp.bfloat16)

            @pl.when(t > 0)
            def _():
                for k in range(heads_axis - 1):
                    share(which, k, t - 1).start()

        for k in range(heads_axis - 1):
            share(which, k, tiles - 1).start()

    def collect(which):
        mine, recv, out, out_hbm = ((fmine, frecv, fout, fo_hbm), (cmine, crecv, cout, co_hbm))[which]

        def put(t):
            at = pl.ds(pl.multiple_of(t * TILE, TILE), TILE)
            return pltpu.make_async_copy(out.at[t], out_hbm.at[:, at], outs.at[which, t])

        @pl.loop(0, tiles)
        def _(t):
            total = mine[t]
            for k in range(heads_axis - 1):
                share(which, k, t).wait_recv()
                total = total + recv[k, t].astype(jnp.float32)
            out[t] = total.astype(jnp.bfloat16)
            put(t).start()

        return put

    facc[...] = jnp.zeros_like(facc)
    cacc[...] = jnp.zeros_like(cacc)
    fstat[...] = jnp.zeros_like(fstat)
    cstat[...] = jnp.zeros_like(cstat)
    fstat[:, 0:1] = jnp.full((fstat.shape[0], 1, fstat.shape[2]), MASKED, jnp.float32)
    cstat[:, 0:1] = jnp.full((cstat.shape[0], 1, cstat.shape[2]), MASKED, jnp.float32)

    greeted = 2 + len(others) + jnp.where(has_right, 1, 0) + jnp.where(has_left, 1, 0)
    pl.semaphore_wait(barrier, greeted)

    first = True
    for kind, which in schedule_of(line, pieces):
        if kind == "O":
            send_own(which[1])
        elif kind == "T":
            take_line(*which)
        elif kind == "U":
            if first:
                w_copy.start()
                for copy in q_copies:
                    copy.wait()

                @pl.loop(0, groups * ratio)
                def _(at):
                    fpair[at] = split_queries(fq[:, columns_of(at)])

                @pl.loop(0, groups * ratio // cstack)
                def _(at):
                    for k in range(cstack):
                        cpair[at, k * crows : (k + 1) * crows] = split_queries(
                            cq[:, columns_of(at * cstack + k)]
                        )

                first = False
            take(*which)
        else:
            finish_coarse()
            w_copy.wait()
            project(1)

    finish_fine()
    project(0)
    cput = collect(1)
    fput = collect(0)

    def done_line(l, way, onward):
        @pl.when(onward)
        def _():
            for a in range(pieces + 1):
                to_line(l, a, way, right if way == 0 else left).wait_send()

    for l in range(line):
        done_line(l, 0, jnp.logical_and(l <= place, has_right))
        done_line(l, 1, jnp.logical_and(l >= place, has_left))
        for a in range(pieces + 1):
            to_pair(l, a).wait_send()
            for q in range(PAIR):
                to_core(l, q, a).wait_send()

    @pl.loop(0, tiles)
    def _(t):
        for k in range(heads_axis - 1):
            share(0, k, t).wait_send()
            share(1, k, t).wait_send()
        cput(t).wait()
        fput(t).wait()


def per_device(mesh_shape, outer, fine_query, fine_memory, coarse_query, coarse_memory, coarse_scale, out_weight):
    heads_axis = mesh_shape["head"]
    line = mesh_shape["ctx"] // (PAIR * CORES)
    rows, width = fine_query.shape
    crows, keys = coarse_query.shape[0], coarse_memory.shape[1]
    groups = coarse_memory.shape[2] // HD
    heads = width // HD
    ratio = heads // groups
    pieces = 1 + fine_memory.shape[1] // keys
    slots = line * PAIR * CORES
    columns = out_weight.shape[1]
    tiles = columns // TILE
    cstack = 2
    part, cpart = rows // heads_axis, crows // heads_axis
    levels = jnp.broadcast_to(coarse_scale.astype(jnp.float32)[None, :], (8, keys))
    f32, bf16 = jnp.float32, jnp.bfloat16
    anywhere = pl.BlockSpec(memory_space=pl.ANY)
    pairs = rows * slots * keys * pieces * heads + crows * slots * keys * heads
    return pl.pallas_call(
        functools.partial(kernel, line, outer, heads_axis, ratio),
        out_shape=(
            jax.ShapeDtypeStruct((part, columns), bf16),
            jax.ShapeDtypeStruct((cpart, columns), bf16),
        ),
        in_specs=[anywhere] * 6,
        out_specs=(anywhere, anywhere),
        scratch_shapes=[
            pltpu.VMEM((pieces, 2, slots * keys, groups * HD), bf16),
            pltpu.VMEM((slots, 8, keys), f32),
            pltpu.VMEM((slots * keys, crows), f32),
            pltpu.VMEM((rows, width), bf16),
            pltpu.VMEM((crows, width), bf16),
            pltpu.VMEM((heads, rows, 2 * HD), bf16),
            pltpu.VMEM((heads // cstack, cstack * crows, 2 * HD), bf16),
            pltpu.VMEM((HD, PAIR * CORES * keys), bf16),
            pltpu.VMEM((heads, HD, rows), f32),
            pltpu.VMEM((heads, 8, rows), f32),
            pltpu.VMEM((heads // cstack, HD, cstack * crows), f32),
            pltpu.VMEM((heads // cstack, 8, cstack * crows), f32),
            pltpu.VMEM((rows, width), bf16),
            pltpu.VMEM((crows, width), bf16),
            pltpu.VMEM(out_weight.shape, bf16),
            pltpu.VMEM((tiles, part, TILE), f32),
            pltpu.VMEM((tiles, cpart, TILE), f32),
            pltpu.VMEM((heads_axis - 1, tiles, part, TILE), bf16),
            pltpu.VMEM((heads_axis - 1, tiles, cpart, TILE), bf16),
            pltpu.VMEM((heads_axis - 1, tiles, part, TILE), bf16),
            pltpu.VMEM((heads_axis - 1, tiles, cpart, TILE), bf16),
            pltpu.VMEM((tiles, part, TILE), bf16),
            pltpu.VMEM((tiles, cpart, TILE), bf16),
            pltpu.SemaphoreType.DMA((line, pieces + 1)),
            pltpu.SemaphoreType.DMA((2, line, pieces + 1)),
            pltpu.SemaphoreType.DMA((line, pieces + 1)),
            pltpu.SemaphoreType.DMA((line, pieces + 1)),
            pltpu.SemaphoreType.DMA((line, PAIR, pieces + 1)),
            pltpu.SemaphoreType.DMA((line, PAIR, pieces + 1)),
            pltpu.SemaphoreType.DMA((2, heads_axis - 1, tiles)),
            pltpu.SemaphoreType.DMA((2, heads_axis - 1, tiles)),
            pltpu.SemaphoreType.DMA((pieces + 4,)),
            pltpu.SemaphoreType.DMA((2, tiles)),
        ],
        compiler_params=pltpu.CompilerParams(
            collective_id=0, has_side_effects=True, vmem_limit_bytes=62 << 20
        ),
        cost_estimate=pl.CostEstimate(
            flops=8 * pairs * HD, transcendentals=pairs, bytes_accessed=4 * rows * width
        ),
    )(fine_query, coarse_query, fine_memory, coarse_memory, levels, out_weight)


def solution(mesh):
    placed = (
        P("ctx", "head"),
        P(None, "ctx", "head"),
        P("ctx", "head"),
        P(None, "ctx", "head"),
        P("ctx"),
        P("head", None),
    )
    return jax.shard_map(
        functools.partial(per_device, dict(mesh.shape), line_is_outer(mesh)),
        mesh=mesh,
        in_specs=placed,
        out_specs=(P(("ctx", "head"), None), P(("ctx", "head"), None)),
        check_vma=False,
    )
```

time: 235 us -> 164 us (0.70)
  waiting for transfers between devices: 103 us -> 0 us
  Pallas kernels: 64.7 us -> 158 us
  blocking collectives: 23.2 us -> 0 us
  matrix products: 20.8 us -> 0 us
  between operations: 13.8 us -> 0.64 us
  local copies, waits for them, and re-layouts: 7.49 us -> 4.75 us
    pallas_call x3 -> x1, Pallas kernels: 64.7 us -> 158 us  [per_device(): pl.pallas_call(functools.partial(kernel, line, outer, heads_axis, ratio),...]
    all_gather x3 -> x0, waiting for transfers between devices: 71.5 us -> none  [gathered(): return lax.all_gather(memory, 'ctx', axis=1, tiled=True)]
    reduce_scatter x2 -> x0, waiting for transfers between devices: 30.6 us -> none  [mix(): lax.psum_scatter(partial.astype(jnp.bfloat16), 'head', scatter_dimension=...]
    all_gather x1 -> x0, blocking collectives: 23.2 us -> none  [per_device(): lax.all_gather(levels.astype(jnp.bfloat16).reshape(1, -1), 'ctx', axis=1,...]
    dot_general x2 -> x0, matrix products: 20.8 us -> none  [mix(): partial = jnp.dot(rows, out_weight, preferred_element_type=jnp.float32)]
    unnamed x10 -> x2, local copies, waits for them, and re-layouts: 5.24 us -> 4.16 us
  transfers between devices with their start and end apart: 5 -> 0, of which waited for: 4 -> 0; matrix products, arithmetic and copies ran while one was open for 10% -> 0% of each run, Pallas kernels for 28% -> 0%
where the time goes in v1:
time: 164 us
  Pallas kernels  158 us (96%)
  local copies, waits for them, and re-layouts  4.75 us (3%)
    pallas_call x1, Pallas kernels, per_device(): pl.pallas_call(functools.partial(kernel, line, outer, heads_axis, ratio),...  158 us
    unnamed x2, local copies, waits for them, and re-layouts  4.16 us

profile of v1, /device:TPU:0, one launch (start us, length us, event | category | flops | bytes accessed | tf_op | source)
XLA Modules:
  0.0 164.1 jit_solution(13387138878459020103)
XLA Ops:
  0.6 0.7 convert_element_type.3
  1.3 0.6 broadcast_in_dim.2.lev_hbm
  1.9 158.0 %shard_map.77 = (bf16[128,4096]{1,0:T(8,128)(2,1)}, bf16[64,4096]{1,0:T(8,128)(2,1)}) custom-call(bf16[256,2048]{1,0:T(8,128)(2,1)} %fq_hbm.1, bf16[128,2048]{1,0:T(8,128)(2,1)} %cq_hbm.1, bf16[2,256,512]{2,1,0:T(8,128)(2,1)} %fm_hbm.1, bf16[2,128,512]{2,1,0:T(8,128)(2,1)} %cm_hbm.1, f32[8,128]{1,0:T(8,128)} %broadcast_in_dim.2.lev_hbm, bf16[2048,4096]{1,0:T(8,128)(2,1)} %w_hbm.1), custom_call_target="tpu_custom_call" | custom-call | flops 30064771072 | bytes 2097152 | tf_op jit(solution)/shard_map/pallas_call | solution.py:464
  159.9 2.3 %copy.10 = bf16[128,4096]{1,0:T(8,128)(2,1)} copy(bf16[128,4096]{1,0:T(8,128)(2,1)} %get-tuple-element.4) | data formatting | bytes 2097152
  162.2 1.9 %copy.11 = bf16[64,4096]{1,0:T(8,128)(2,1)} copy(bf16[64,4096]{1,0:T(8,128)(2,1)} %get-tuple-element.5) | data formatting | bytes 1048576
